TPU v7x, 32 devices: a whole 2x2x4 slice. The times are simulated.
32 devices in a mesh: groups: 2 (over y), latent: 4 (over z), rows: 4 (over x, core).
Axes of the slice: x: 2, y: 2, z: 4, core: 2. Of those that a mesh axis runs over, the one named last changes fastest.
Arguments:
- activations_in: bfloat16 [2, 128, 2304], P('groups', None, 'latent'), parts along dimension 0, may hold values from -6 to 6
- gate_proj: bfloat16 [2304, 4608], P('rows', 'latent'), may hold values from -0.125 to 0.125
- up_proj: bfloat16 [2304, 4608], P('rows', 'latent'), may hold values from -0.125 to 0.125
- down_proj: bfloat16 [4608, 2304], P('latent', 'rows'), may hold values from -0.09375 to 0.09375
- enc_weight: bfloat16 [4608, 65536], P(('groups', 'rows'), 'latent'), parts along dimension 0, may hold values from -6 to 6
- enc_bias: float32 [131072], P(('groups', 'latent')), parts along dimension 0, may hold values from -0.5 to 0.5
- dec_weight: bfloat16 [131072, 2304], P(('groups', 'latent'), 'rows'), parts along dimension 0, may hold values from -6 to 6
- dec_bias: float32 [4608], P(('groups', 'rows')), parts along dimension 0, may hold values from -0.5 to 0.5
Outputs:
- enc_weight_new: bfloat16 [4608, 65536], P(('groups', 'rows'), 'latent'), parts along dimension 0
- enc_bias_new: float32 [131072], P(('groups', 'latent')), parts along dimension 0
- dec_weight_new: bfloat16 [131072, 2304], P(('groups', 'latent'), 'rows'), parts along dimension 0
- dec_bias_new: float32 [4608], P(('groups', 'rows')), parts along dimension 0
There are 2 independent parts, one for each index of `groups`. A program takes and returns all parts, laid end to end along the dimension named above; an argument that names none is the same for every part. Nothing has to cross between parts.
All inputs are finite; a program needn't handle non-finite values.
Results may differ from a plain program's by a relative error of at most 0.02.
Values may be sent and summed in bfloat16 or wider, within the bound.
A program may use at most 128 MiB of HBM per device.

v0:
```python
import jax
import jax.numpy as jnp
from jax import lax
from jax.sharding import PartitionSpec as P

MODEL_WIDTH = 2304
LATENTS = 65536
sparsity_cost = 0.1
sharpness = 8.0
weight_rate = 2.0
enc_bias_rate = 0.01
dec_bias_rate = 0.002


def row_total(term):
    return lax.psum(term.astype(jnp.bfloat16), "rows").astype(jnp.float32)


def body(activations_in, gate_proj, up_proj, down_proj, enc_weight, enc_bias, dec_weight, dec_bias):
    gate_full, up_full = (
        lax.all_gather(gate_proj, "rows", axis=0, tiled=True),
        lax.all_gather(up_proj, "rows", axis=0, tiled=True),
    )
    batches = activations_in.shape[0]
    batch_tokens = activations_in.shape[1]
    all_tokens = batches * batch_tokens
    token_rows = activations_in.reshape(all_tokens, activations_in.shape[2])
    portion = lax.all_gather(token_rows, "latent", axis=1, tiled=True)
    gate_term = jnp.dot(portion, gate_full, preferred_element_type=jnp.float32)
    up_term = jnp.dot(portion, up_full, preferred_element_type=jnp.float32)
    hidden = (jax.nn.gelu(gate_term, approximate=True) * up_term).astype(jnp.bfloat16)
    partial_value = jnp.dot(hidden, down_proj, preferred_element_type=jnp.float32)
    features = lax.psum(partial_value, "latent").astype(jnp.bfloat16)
    features = features.reshape(batches, batch_tokens, features.shape[1])
    enc_scale = MODEL_WIDTH ** (-0.5)
    dec_scale = LATENTS ** (-0.5)
    inputs = features[0]
    local_pre = jnp.dot(inputs, enc_weight, preferred_element_type=jnp.float32)
    pre_latent = enc_scale * row_total(local_pre) + enc_bias
    latents = (jax.nn.softplus(sharpness * pre_latent) / sharpness).astype(jnp.bfloat16)
    local_rebuilt = jnp.dot(latents, dec_weight, preferred_element_type=jnp.float32)
    rebuilt_share = lax.psum_scatter(local_rebuilt, "latent", scatter_dimension=1, tiled=True)
    share_cols = rebuilt_share.shape[1]
    col_offset = lax.axis_index("latent") * share_cols
    inputs_here = lax.dynamic_slice_in_dim(inputs, col_offset, share_cols, 1)
    bias_here = lax.dynamic_slice_in_dim(dec_bias, col_offset, share_cols, 0)
    grad_share = (
        2.0 * (dec_scale * rebuilt_share + bias_here - inputs_here.astype(jnp.float32))
    ).astype(jnp.bfloat16)
    residual_grad = lax.all_gather(grad_share, "latent", axis=1, tiled=True)
    local_back = lax.dot_general(
        residual_grad, dec_weight, (((1,), (1,)), ((), ())), preferred_element_type=jnp.float32
    )
    back_sum = row_total(local_back)
    latent_grad = (
        jax.nn.sigmoid(sharpness * pre_latent) * (dec_scale * back_sum + sparsity_cost)
    ).astype(jnp.bfloat16)
    dec_grad = dec_scale * lax.dot_general(
        latents, residual_grad, (((0,), (0,)), ((), ())), preferred_element_type=jnp.float32
    )
    enc_grad = enc_scale * lax.dot_general(
        inputs, latent_grad, (((0,), (0,)), ((), ())), preferred_element_type=jnp.float32
    )
    enc_bias = enc_bias - enc_bias_rate * jnp.sum(latent_grad, axis=0, dtype=jnp.float32)
    dec_bias = dec_bias - dec_bias_rate * jnp.sum(residual_grad, axis=0, dtype=jnp.float32)
    enc_weight = (enc_weight.astype(jnp.float32) - weight_rate * enc_grad).astype(jnp.bfloat16)
    dec_weight = (dec_weight.astype(jnp.float32) - weight_rate * dec_grad).astype(jnp.bfloat16)
    return (enc_weight, enc_bias, dec_weight, dec_bias)


def solution(mesh):
    return jax.shard_map(
        body,
        mesh=mesh,
        in_specs=(
            P("groups", None, "latent"),
            P("rows", "latent"),
            P("rows", "latent"),
            P("latent", "rows"),
            P(("groups", "rows"), "latent"),
            P(("groups", "latent")),
            P(("groups", "latent"), "rows"),
            P(("groups", "rows")),
        ),
        out_specs=(
            P(("groups", "rows"), "latent"),
            P(("groups", "latent")),
            P(("groups", "latent"), "rows"),
            P(("groups", "rows")),
        ),
        check_vma=False,
    )
```

profile of v0, /device:TPU:0, one launch (start us, length us, event | category | flops | bytes accessed | tf_op | source)
XLA Modules:
  0.0 395.9 jit_solution(4908214912626969955)
XLA Ops:
  7.2 0.0 copy-start
  7.2 0.0 all-gather.4.cloned.1.call-start
  7.2 0.7 all-gather.4.cloned.1.call-update
  7.9 0.0 all-gather.6.cloned.1.call-start
  8.0 0.7 all-gather.6.cloned.1.call-update
  8.7 0.0 all-reduce.4.cloned.1.call-start
  8.7 18.5 %all-gather = bf16[1,128,2304]{1,2,0:T(8,128)(2,1)S(1)} all-gather(bf16[1,128,576]{1,2,0:T(8,128)(2,1)} %param.8), channel_id=2, replica_groups=mesh['groups'=2,'latent'=4,'rows'=4] {'latent'}, dimensions={2}, use_global_device_ids=true | all-gather | bytes 737280 | tf_op jit(solution)/shard_map/all_gather | solution.py:28
  27.2 25.9 %all-gather.4.cloned.1.call-done = bf16[2304,1152]{1,0:T(8,128)(2,1)} async-done(((bf16[576,1152]{1,0:T(8,128)(2,1)}), bf16[2304,1152]{1,0:T(8,128)(2,1)}) %all-gather.4.cloned.1.call-update) | async-done | bytes 5308432 | tf_op jit(solution)/shard_map/all_gather | solution.py:21
  53.1 3.5 fusion.14
  56.6 38.9 %all-gather.6.cloned.1.call-done = bf16[2304,1152]{1,0:T(8,128)(2,1)} async-done(((bf16[576,1152]{1,0:T(8,128)(2,1)}), bf16[2304,1152]{1,0:T(8,128)(2,1)}) %all-gather.6.cloned.1.call-update) | async-done | bytes 5308432 | tf_op jit(solution)/shard_map/all_gather | solution.py:22
  95.5 0.0 copy-done
  95.5 4.0 fusion.3
  99.4 25.3 %all-reduce.7 = bf16[128,576]{0,1:T(8,128)(2,1)S(1)} all-reduce(f32[128,576]{0,1:T(8,128)S(1)} %fusion.3), channel_id=1, replica_groups=mesh['groups'=2,'latent'=4,'rows'=4] {'latent'}, use_global_device_ids=true, to_apply=%region_0.0 | all-reduce | flops 73728 | bytes 442368 | tf_op jit(solution)/shard_map/psum | solution.py:33
  124.7 0.0 copy-start.2
  124.8 12.0 %convolution_convert_fusion.1 = bf16[128,16384]{1,0:T(8,128)(2,1)} fusion(bf16[128,576]{0,1:T(8,128)(2,1)S(1)} %all-reduce.7, bf16[576,16384]{1,0:T(8,128)(2,1)} %param.12), kind=kOutput, calls=%fused_computation.4 | convolution fusion | flops 2418016256 | bytes 23216128 | tf_op jit(solution)/shard_map/dot_general | solution.py:38
  136.7 0.0 all-reduce.4.cloned.1.call-update
  136.8 0.0 copy-start.3
  136.8 0.2 reduce-scatter.2.cloned.1.call-start
  137.0 82.7 %all-reduce.4.cloned.1.call-done = bf16[128,16384]{1,0:T(8,128)(2,1)} async-done(((bf16[128,16384]{1,0:T(8,128)(2,1)}), bf16[128,16384]{1,0:T(8,128)(2,1)}) %all-reduce.4.cloned.1.call-update) | async-done | bytes 4194320 | tf_op jit(solution)/shard_map/psum | solution.py:16
  219.7 0.0 copy-done.2
  219.7 15.9 %fusion.25 = f32[128,576]{0,1:T(8,128)} fusion(bf16[16384,576]{0,1:T(8,128)(2,1)} %param.14, bf16[128,16384]{1,0:T(8,128)(2,1)} %all-reduce.4.cloned.1.call-done, f32[16384]{0:T(1024)S(1)} %copy-done.2), kind=kOutput, calls=%fused_computation.36 | convolution fusion | flops 2441084928 | bytes 23429120 | tf_op jit(solution)/shard_map/dot_general | solution.py:41
  235.6 0.0 reduce-scatter.2.cloned.1.call-update
  235.6 0.0 all-reduce.6.cloned.1.call-start
  235.7 0.0 copy-done.3
  235.7 0.1 dynamic_slice.6
  235.8 20.4 %reduce-scatter.2.cloned.1.call-done = f32[128,144]{0,1:T(8,128)} async-done(((f32[128,576]{0,1:T(8,128)}), f32[128,144]{0,1:T(8,128)}) %reduce-scatter.2.cloned.1.call-update) | async-done | bytes 73744 | tf_op jit(solution)/shard_map/reduce_scatter | solution.py:42
  256.2 1.0 multiply_convert_fusion.1
  257.1 13.5 %all_gather.15 = bf16[128,576]{0,1:T(8,128)(2,1)S(1)} all-gather(bf16[128,144]{0,1:T(8,128)(2,1)S(1)} %multiply_convert_fusion.1), channel_id=1, replica_groups=mesh['groups'=2,'latent'=4,'rows'=4] {'latent'}, dimensions={1}, use_global_device_ids=true | all-gather | bytes 184320 | tf_op jit(solution)/shard_map/all_gather | solution.py:50
  270.6 12.0 %convolution_convert_fusion = bf16[128,16384]{1,0:T(8,128)(2,1)} fusion(bf16[128,576]{0,1:T(8,128)(2,1)S(1)} %all_gather.15, bf16[16384,576]{0,1:T(8,128)(2,1)} %param.14), kind=kOutput, calls=%fused_computation.3 | convolution fusion | flops 2418016256 | bytes 23216128 | tf_op jit(solution)/shard_map/dot_general | solution.py:51
  282.6 0.1 convert_reduce_fusion.1
  282.7 0.0 all-reduce.6.cloned.1.call-update
  282.7 0.6 multiply_subtract_fusion.1
  283.3 32.5 %subtract_convert_fusion = bf16[16384,576]{0,1:T(8,128)(2,1)} fusion(bf16[16384,576]{0,1:T(8,128)(2,1)} %param.14, bf16[128,576]{0,1:T(8,128)(2,1)S(1)} %all_gather.15, bf16[128,16384]{1,0:T(8,128)(2,1)} %all-reduce.4.cloned.1.call-done, f32[16384]{0:T(1024)S(1)} %copy-done.2), kind=kOutput, calls=%fused_computation | convolution fusion | flops 2478833664 | bytes 42156032 | tf_op jit(solution)/shard_map/dot_general | solution.py:58
  315.8 50.7 %all-reduce.6.cloned.1.call-done = bf16[128,16384]{1,0:T(8,128)(2,1)} async-done(((bf16[128,16384]{1,0:T(8,128)(2,1)}), bf16[128,16384]{1,0:T(8,128)(2,1)}) %all-reduce.6.cloned.1.call-update) | async-done | bytes 4194320 | tf_op jit(solution)/shard_map/psum | solution.py:16
  366.5 7.7 %convert_reduce_fusion = (f32[16384]{0:T(1024)S(1)}, bf16[128,16384]{1,0:T(8,128)(2,1)}) fusion(bf16[128,16384]{1,0:T(8,128)(2,1)} %all-reduce.6.cloned.1.call-done, f32[16384]{0:T(1024)S(1)} %copy-done.2, bf16[128,16384]{1,0:T(8,128)(2,1)} %all-reduce.4.cloned.1.call-done), kind=kLoop, calls=%fused_computation.7 | loop fusion | flops 29343744 | bytes 12713984 | tf_op jit(solution)/shard_map/reduce_sum | solution.py:64
  374.2 0.0 copy-start.1
  374.2 14.5 %subtract_convert_fusion.1 = bf16[576,16384]{1,0:T(8,128)(2,1)} fusion(bf16[576,16384]{1,0:T(8,128)(2,1)} %param.12, bf16[128,576]{0,1:T(8,128)(2,1)S(1)} %all-reduce.7, bf16[128,16384]{1,0:T(8,128)(2,1)} %get-tuple-element.5), kind=kOutput, calls=%fused_computation.1 | convolution fusion | flops 2453667840 | bytes 42090496 | tf_op jit(solution)/shard_map/dot_general | solution.py:61
  388.7 0.6 multiply_subtract_fusion
  389.3 0.0 copy-done.1
Async XLA Ops:
  7.2 88.3 %copy-start = (bf16[1152,576]{0,1:T(8,128)(2,1)S(1)}, bf16[1152,576]{0,1:T(8,128)(2,1)}, u32[]{:S(2)}) copy-start(bf16[1152,576]{0,1:T(8,128)(2,1)} %param.11) | copy-start | bytes 3981316
  7.2 45.9 %all-gather.4.cloned.1.call-start = ((), (), s32[]{:S(2)}) async-start(), calls=%async_computation.1 | async-start | bytes 6635520 | tf_op jit(solution)/shard_map/all_gather | solution.py:21
  7.9 87.5 %all-gather.6.cloned.1.call-start = ((), (), s32[]{:S(2)}) async-start(), calls=%async_computation.2 | async-start | bytes 6635520 | tf_op jit(solution)/shard_map/all_gather | solution.py:22
  8.7 211.0 %all-reduce.4.cloned.1.call-start = ((), (), s32[]{:S(2)}) async-start(), calls=%async_computation.3 | async-start | bytes 8388608 | tf_op jit(solution)/shard_map/psum | solution.py:16
  124.7 94.9 %copy-start.2 = (f32[16384]{0:T(1024)S(1)}, f32[16384]{0:T(1024)}, u32[]{:S(2)}) copy-start(f32[16384]{0:T(1024)} %param.13) | copy-start | bytes 196612
  136.8 98.9 %copy-start.3 = (f32[576]{0:T(1024)S(1)}, f32[576]{0:T(1024)}, u32[]{:S(2)}) copy-start(f32[576]{0:T(1024)} %param.15) | copy-start | bytes 6916
  136.8 119.4 %reduce-scatter.2.cloned.1.call-start = ((), (), s32[]{:S(2)}) async-start(), calls=%async_computation.4 | async-start | bytes 368640 | tf_op jit(solution)/shard_map/reduce_scatter | solution.py:42
  235.6 130.9 %all-reduce.6.cloned.1.call-start = ((), (), s32[]{:S(2)}) async-start(), calls=%async_computation.5 | async-start | bytes 8388608 | tf_op jit(solution)/shard_map/psum | solution.py:16
  374.2 15.1 %copy-start.1 = (bf16[1152,576]{0,1:T(8,128)(2,1)S(1)}, bf16[1152,576]{0,1:T(8,128)(2,1)}, u32[]{:S(2)}) copy-start(bf16[1152,576]{0,1:T(8,128)(2,1)} %param.11) | copy-start | bytes 3981316
Sparse Core Ops, SparseCore 0:
  9.5 43.4 all-gather.3
  54.6 40.7 all-gather.5
  136.9 82.7 all-reduce.3
  235.8 20.3 reduce-scatter.1
  282.9 83.6 all-reduce.5
where the time goes:
time: 396 us
  waiting for transfers between devices  220 us (56%)
  matrix products  94.3 us (24%)
  blocking collectives  57.3 us (14%)
  between operations  13.8 us (3%)
  other arithmetic  10 us (3%)
    psum x2, waiting for transfers between devices, row_total(): return lax.psum(term.astype(jnp.bfloat16), 'rows').astype(jnp.float32)  133 us
    all_gather x1, waiting for transfers between devices, body(): lax.all_gather(up_proj, 'rows', axis=0, tiled=True)  38.9 us
    dot_general x1, matrix products, body(): lax.dot_general(latents, residual_grad, (((0,), (0,)), ((), ())), preferr...  32.5 us
    all_gather x1, waiting for transfers between devices, body(): lax.all_gather(gate_proj, 'rows', axis=0, tiled=True)  25.9 us
    psum x1, blocking collectives, body(): features = lax.psum(partial_value, 'latent').astype(jnp.bfloat16)  25.3 us
    reduce_scatter x1, waiting for transfers between devices, body(): lax.psum_scatter(local_rebuilt, 'latent', scatter_dimension=1, tiled=True)  20.4 us
    all_gather x1, blocking collectives, body(): portion = lax.all_gather(token_rows, 'latent', axis=1, tiled=True)  18.5 us
    dot_general x1, matrix products, body(): jnp.dot(latents, dec_weight, preferred_element_type=jnp.float32)  15.9 us
  transfers between devices with their start and end apart: 5, of which 5 were waited for; matrix products, arithmetic and copies ran while one was open for 9% of the time, Pallas kernels for 0%

commit v1 on v0

--- a/solution.py
+++ b/solution.py
@@ -1,7 +1,9 @@
+import functools
 import jax
 import jax.numpy as jnp
 from jax import lax
 from jax.sharding import PartitionSpec as P
+from jax.lax import axis_index, axis_size, ppermute
 
 MODEL_WIDTH = 2304
 LATENTS = 65536
@@ -12,6 +14,27 @@
 dec_bias_rate = 0.002
 
 
+def _do_meshes(arr, along_dim):
+    gallery = []
+    cores_n = axis_size("rows")
+    for t in range(cores_n):
+        gallery.append((t, (t + 1) % cores_n))
+    pile = []
+    for t in range(cores_n):
+        pile.append((t, (t - 1) % cores_n))
+    y2, lower = ([arr], [arr])
+    for _ in range(cores_n // 2):
+        fresh = ppermute(y2[-1], "rows", gallery)
+        y2.append(fresh)
+    for _ in range((cores_n - 1) // 2):
+        lower.append(ppermute(lower[-1], "rows", pile))
+    inter = jnp.concatenate([*y2[::-1], *lower[1:]], along_dim)
+    return jnp.roll(inter, (axis_index("rows") - cores_n // 2) * arr.shape[along_dim], along_dim)
+
+
+_number_screen = functools.partial(_do_meshes, along_dim=0)
+
+
 def row_total(term):
     return lax.psum(term.astype(jnp.bfloat16), "rows").astype(jnp.float32)
 
@@ -19,7 +42,7 @@
 def body(activations_in, gate_proj, up_proj, down_proj, enc_weight, enc_bias, dec_weight, dec_bias):
     gate_full, up_full = (
         lax.all_gather(gate_proj, "rows", axis=0, tiled=True),
-        lax.all_gather(up_proj, "rows", axis=0, tiled=True),
+        _number_screen(up_proj),
     )
     batches = activations_in.shape[0]
     batch_tokens = activations_in.shape[1]

time: 396 us -> 407 us (1.028)
  local copies, waits for them, and re-layouts: 0.11 us -> 18.7 us
  waiting for transfers between devices: 220 us -> 205 us
  starting transfers between devices: 0.38 us -> 4.82 us
    ppermute x0 -> x3, waiting for transfers between devices: none -> 50.4 us  [the longest x2 50.4 us: _do_meshes(): fresh = ppermute(y2[-1], 'rows', gallery)]
    all_gather x1 -> x0, waiting for transfers between devices: 38.9 us -> none  [body(): lax.all_gather(up_proj, 'rows', axis=0, tiled=True)]
    all_gather x1, waiting for transfers between devices: 25.9 us -> 0.01 us  [body(): lax.all_gather(gate_proj, 'rows', axis=0, tiled=True)]
    unnamed x8 -> x17, local copies, waits for them, and re-layouts: 0.03 us -> 16.1 us
    ppermute x0 -> x3, starting transfers between devices: none -> 4.48 us  [the longest x2 4.48 us: _do_meshes(): fresh = ppermute(y2[-1], 'rows', gallery)]
  transfers between devices with their start and end apart: 5 -> 7, of which waited for: 5 -> 5; matrix products, arithmetic and copies ran while one was open for 9% -> 13% of each run, Pallas kernels for 0% -> 0%
where the time goes in v1:
time: 407 us; the launch traced here: 406 us
  waiting for transfers between devices  205 us (50%)
  matrix products  95 us (23%)
  blocking collectives  59.1 us (15%)
  local copies, waits for them, and re-layouts  18.7 us (5%)
  between operations  13.9 us (3%)
  other arithmetic  9.97 us (2%)
  starting transfers between devices  4.82 us (1%)
    psum x2, waiting for transfers between devices, row_total(): return lax.psum(term.astype(jnp.bfloat16), 'rows').astype(jnp.float32)  133 us
    ppermute x2, waiting for transfers between devices, _do_meshes(): fresh = ppermute(y2[-1], 'rows', gallery)  50.4 us
    dot_general x1, matrix products, body(): lax.dot_general(latents, residual_grad, (((0,), (0,)), ((), ())), preferr...  32.5 us
    psum x1, blocking collectives, body(): features = lax.psum(partial_value, 'latent').astype(jnp.bfloat16)  27.5 us
    reduce_scatter x1, waiting for transfers between devices, body(): lax.psum_scatter(local_rebuilt, 'latent', scatter_dimension=1, tiled=True)  20.4 us
    all_gather x1, blocking collectives, body(): portion = lax.all_gather(token_rows, 'latent', axis=1, tiled=True)  18.1 us
    unnamed x17, local copies, waits for them, and re-layouts  16.1 us
    dot_general x1, matrix products, body(): jnp.dot(latents, dec_weight, preferred_element_type=jnp.float32)  15.9 us
  transfers between devices with their start and end apart: 7, of which 5 were waited for; matrix products, arithmetic and copies ran while one was open for 13% of the time, Pallas kernels for 0%

profile of v1, /device:TPU:0, one launch (start us, length us, event | category | flops | bytes accessed | tf_op | source)
XLA Modules:
  0.0 406.4 jit_solution(17516812404903544010)
XLA Ops:
  7.2 0.0 copy-start
  7.2 0.0 all-gather.3.cloned.1.call-start
  7.2 0.7 all-gather.3.cloned.1.call-update
  7.9 0.0 copy-start.2
  7.9 0.0 all-reduce.4.cloned.1.call-start
  8.0 0.5 collective-permute-start
  8.5 23.8 %collective-permute-done = bf16[576,1152]{1,0:T(8,128)(2,1)} collective-permute-done((bf16[576,1152]{1,0:T(8,128)(2,1)}, bf16[576,1152]{1,0:T(8,128)(2,1)}, u32[]{:S(2)}, u32[]{:S(2)}) %collective-permute-start) | collective-permute-done | bytes 1327136 | tf_op jit(solution)/shard_map/ppermute | solution.py:27
  32.3 3.9 collective-permute-start.1
  36.3 0.0 collective-permute-start.2
  36.3 18.1 %all-gather = bf16[1,128,2304]{1,2,0:T(8,128)(2,1)S(1)} all-gather(bf16[1,128,576]{1,2,0:T(8,128)(2,1)} %param.8), channel_id=2, replica_groups=mesh['groups'=2,'latent'=4,'rows'=4] {'latent'}, dimensions={2}, use_global_device_ids=true | all-gather | bytes 737280 | tf_op jit(solution)/shard_map/all_gather | solution.py:51
  54.4 26.6 %collective-permute-done.1 = bf16[576,1152]{1,0:T(8,128)(2,1)} collective-permute-done((bf16[576,1152]{1,0:T(8,128)(2,1)}, bf16[576,1152]{1,0:T(8,128)(2,1)}, u32[]{:S(2)}, u32[]{:S(2)}) %collective-permute-start.1) | collective-permute-done | bytes 1327136 | tf_op jit(solution)/shard_map/ppermute | solution.py:27
  80.9 2.5 constant_dynamic-update-slice_fusion.7
  83.4 2.5 constant_dynamic-update-slice_fusion.6
  85.9 2.5 constant_dynamic-update-slice_fusion.5
  88.4 0.0 collective-permute-done.2
  88.4 2.5 constant_dynamic-update-slice_fusion.4
  90.9 2.5 constant_dynamic-update-slice_fusion.3
  93.4 2.5 constant_dynamic-update-slice_fusion.2
  95.9 0.0 copy-done.2
  95.9 1.2 constant_dynamic-update-slice_fusion.1
  97.0 2.5 constant_dynamic-update-slice_fusion
  99.5 0.0 all-gather.3.cloned.1.call-done
  99.5 3.5 fusion.26
  103.0 0.0 copy-done
  103.0 4.7 %fusion.14 = f32[128,576]{0,1:T(8,128)S(1)} fusion(bf16[1152,576]{0,1:T(8,128)(2,1)S(1)} %copy-done, bf16[4608,1152]{1,0:T(8,128)(2,1)} %constant_dynamic-update-slice_fusion, s32[]{:T(128)S(6)} %select_n.22, f32[128,1152]{1,0:T(8,128)S(1)} %fusion.26, bf16[1,128,2304]{1,2,0:T(8,128)(2,1)S(1)} %all-gather), kind=kOutput, calls=%fused_computation.15 | convolution fusion | flops 850821120 | bytes 8110084 | tf_op jit(solution)/shard_map/dot_general | solution.py:55
  107.6 27.5 %all-reduce.7 = bf16[128,576]{0,1:T(8,128)(2,1)S(1)} all-reduce(f32[128,576]{0,1:T(8,128)S(1)} %fusion.14), channel_id=1, replica_groups=mesh['groups'=2,'latent'=4,'rows'=4] {'latent'}, use_global_device_ids=true, to_apply=%region_0.1 | all-reduce | flops 73728 | bytes 442368 | tf_op jit(solution)/shard_map/psum | solution.py:56
  135.2 0.0 copy-start.3
  135.2 12.0 %convolution_convert_fusion.1 = bf16[128,16384]{1,0:T(8,128)(2,1)} fusion(bf16[128,576]{0,1:T(8,128)(2,1)S(1)} %all-reduce.7, bf16[576,16384]{1,0:T(8,128)(2,1)} %param.12), kind=kOutput, calls=%fused_computation.4 | convolution fusion | flops 2418016256 | bytes 23216128 | tf_op jit(solution)/shard_map/dot_general | solution.py:61
  147.2 0.0 all-reduce.4.cloned.1.call-update
  147.2 0.0 copy-start.4
  147.2 0.2 reduce-scatter.2.cloned.1.call-start
  147.4 82.8 %all-reduce.4.cloned.1.call-done = bf16[128,16384]{1,0:T(8,128)(2,1)} async-done(((bf16[128,16384]{1,0:T(8,128)(2,1)}), bf16[128,16384]{1,0:T(8,128)(2,1)}) %all-reduce.4.cloned.1.call-update) | async-done | bytes 4194320 | tf_op jit(solution)/shard_map/psum | solution.py:39
  230.2 0.0 copy-done.3
  230.3 15.9 %fusion.39 = f32[128,576]{0,1:T(8,128)} fusion(bf16[16384,576]{0,1:T(8,128)(2,1)} %param.14, bf16[128,16384]{1,0:T(8,128)(2,1)} %all-reduce.4.cloned.1.call-done, f32[16384]{0:T(1024)S(1)} %copy-done.3), kind=kOutput, calls=%fused_computation.48 | convolution fusion | flops 2441084928 | bytes 23429120 | tf_op jit(solution)/shard_map/dot_general | solution.py:64
  246.2 0.0 reduce-scatter.2.cloned.1.call-update
  246.2 0.0 all-reduce.6.cloned.1.call-start
  246.3 0.0 copy-done.4
  246.3 0.1 dynamic_slice.11
  246.3 20.4 %reduce-scatter.2.cloned.1.call-done = f32[128,144]{0,1:T(8,128)} async-done(((f32[128,576]{0,1:T(8,128)}), f32[128,144]{0,1:T(8,128)}) %reduce-scatter.2.cloned.1.call-update) | async-done | bytes 73744 | tf_op jit(solution)/shard_map/reduce_scatter | solution.py:65
  266.7 1.0 multiply_convert_fusion.1
  267.7 13.5 %all_gather.11 = bf16[128,576]{0,1:T(8,128)(2,1)S(1)} all-gather(bf16[128,144]{0,1:T(8,128)(2,1)S(1)} %multiply_convert_fusion.1), channel_id=1, replica_groups=mesh['groups'=2,'latent'=4,'rows'=4] {'latent'}, dimensions={1}, use_global_device_ids=true | all-gather | bytes 184320 | tf_op jit(solution)/shard_map/all_gather | solution.py:73
  281.2 12.0 %convolution_convert_fusion = bf16[128,16384]{1,0:T(8,128)(2,1)} fusion(bf16[128,576]{0,1:T(8,128)(2,1)S(1)} %all_gather.11, bf16[16384,576]{0,1:T(8,128)(2,1)} %param.14), kind=kOutput, calls=%fused_computation.3 | convolution fusion | flops 2418016256 | bytes 23216128 | tf_op jit(solution)/shard_map/dot_general | solution.py:74
  293.1 0.1 convert_reduce_fusion.1
  293.3 0.0 all-reduce.6.cloned.1.call-update
  293.3 0.6 multiply_subtract_fusion.1
  293.9 32.5 %subtract_convert_fusion = bf16[16384,576]{0,1:T(8,128)(2,1)} fusion(bf16[16384,576]{0,1:T(8,128)(2,1)} %param.14, bf16[128,576]{0,1:T(8,128)(2,1)S(1)} %all_gather.11, bf16[128,16384]{1,0:T(8,128)(2,1)} %all-reduce.4.cloned.1.call-done, f32[16384]{0:T(1024)S(1)} %copy-done.3), kind=kOutput, calls=%fused_computation | convolution fusion | flops 2478833664 | bytes 42156032 | tf_op jit(solution)/shard_map/dot_general | solution.py:81
  326.4 50.7 %all-reduce.6.cloned.1.call-done = bf16[128,16384]{1,0:T(8,128)(2,1)} async-done(((bf16[128,16384]{1,0:T(8,128)(2,1)}), bf16[128,16384]{1,0:T(8,128)(2,1)}) %all-reduce.6.cloned.1.call-update) | async-done | bytes 4194320 | tf_op jit(solution)/shard_map/psum | solution.py:39
  377.1 7.6 %convert_reduce_fusion = (f32[16384]{0:T(1024)S(1)}, bf16[128,16384]{1,0:T(8,128)(2,1)}) fusion(bf16[128,16384]{1,0:T(8,128)(2,1)} %all-reduce.6.cloned.1.call-done, f32[16384]{0:T(1024)S(1)} %copy-done.3, bf16[128,16384]{1,0:T(8,128)(2,1)} %all-reduce.4.cloned.1.call-done), kind=kLoop, calls=%fused_computation.7 | loop fusion | flops 29343744 | bytes 12713984 | tf_op jit(solution)/shard_map/reduce_sum | solution.py:87
  384.7 0.0 copy-start.1
  384.7 14.5 %subtract_convert_fusion.1 = bf16[576,16384]{1,0:T(8,128)(2,1)} fusion(bf16[576,16384]{1,0:T(8,128)(2,1)} %param.12, bf16[128,576]{0,1:T(8,128)(2,1)S(1)} %all-reduce.7, bf16[128,16384]{1,0:T(8,128)(2,1)} %get-tuple-element.5), kind=kOutput, calls=%fused_computation.1 | convolution fusion | flops 2453667840 | bytes 42090496 | tf_op jit(solution)/shard_map/dot_general | solution.py:84
  399.2 0.6 multiply_subtract_fusion
  399.9 0.0 copy-done.1
Async XLA Ops:
  7.2 95.8 %copy-start = (bf16[1152,576]{0,1:T(8,128)(2,1)S(1)}, bf16[1152,576]{0,1:T(8,128)(2,1)}, u32[]{:S(2)}) copy-start(bf16[1152,576]{0,1:T(8,128)(2,1)} %param.11) | copy-start | bytes 3981316
  7.2 92.3 %all-gather.3.cloned.1.call-start = ((), (), s32[]{:S(2)}) async-start(), calls=%async_computation.1 | async-start | bytes 6635520 | tf_op jit(solution)/shard_map/all_gather | solution.py:44
  7.9 87.9 %copy-start.2 = (bf16[576,1152]{1,0:T(8,128)(2,1)S(1)}, bf16[576,1152]{1,0:T(8,128)(2,1)}, u32[]{:S(2)}) copy-start(bf16[576,1152]{1,0:T(8,128)(2,1)} %param.10) | copy-start | bytes 3981316
  7.9 222.3 %all-reduce.4.cloned.1.call-start = ((), (), s32[]{:S(2)}) async-start(), calls=%async_computation.2 | async-start | bytes 8388608 | tf_op jit(solution)/shard_map/psum | solution.py:39
  8.0 24.4 %collective-permute-start = (bf16[576,1152]{1,0:T(8,128)(2,1)}, bf16[576,1152]{1,0:T(8,128)(2,1)}, u32[]{:S(2)}, u32[]{:S(2)}) collective-permute-start(bf16[576,1152]{1,0:T(8,128)(2,1)} %param.10), channel_id=1, source_target_pairs={{0,1},{1,2},{2,3},{3,0},{4,5},{5,6},{6,7},{7,4},{8,9},{9,10},{10,1... | collective-permute-start | bytes 3981320 | tf_op jit(solution)/shard_map/ppermute | solution.py:27
  32.3 48.6 %collective-permute-start.1 = (bf16[576,1152]{1,0:T(8,128)(2,1)}, bf16[576,1152]{1,0:T(8,128)(2,1)}, u32[]{:S(2)}, u32[]{:S(2)}) collective-permute-start(bf16[576,1152]{1,0:T(8,128)(2,1)} %collective-permute-done), channel_id=1, source_target_pairs={{0,1},{1,2},{2,3},{3,0},{4,5},{5,6},{6,7},{7,4},{8,9},{9,10},{10,1... | collective-permute-start | bytes 3981320 | tf_op jit(solution)/shard_map/ppermute | solution.py:27
  36.3 52.1 %collective-permute-start.2 = (bf16[576,1152]{1,0:T(8,128)(2,1)}, bf16[576,1152]{1,0:T(8,128)(2,1)}, u32[]{:S(2)}, u32[]{:S(2)}) collective-permute-start(bf16[576,1152]{1,0:T(8,128)(2,1)} %param.10), channel_id=1, source_target_pairs={{0,3},{1,0},{2,1},{3,2},{4,7},{5,4},{6,5},{7,6},{8,11},{9,8},{10,9... | collective-permute-start | bytes 3981320 | tf_op jit(solution)/shard_map/ppermute | solution.py:30
  135.2 95.1 %copy-start.3 = (f32[16384]{0:T(1024)S(1)}, f32[16384]{0:T(1024)}, u32[]{:S(2)}) copy-start(f32[16384]{0:T(1024)} %param.13) | copy-start | bytes 196612
  147.2 99.1 %copy-start.4 = (f32[576]{0:T(1024)S(1)}, f32[576]{0:T(1024)}, u32[]{:S(2)}) copy-start(f32[576]{0:T(1024)} %param.15) | copy-start | bytes 6916
  147.2 119.5 %reduce-scatter.2.cloned.1.call-start = ((), (), s32[]{:S(2)}) async-start(), calls=%async_computation.3 | async-start | bytes 368640 | tf_op jit(solution)/shard_map/reduce_scatter | solution.py:65
  246.2 130.9 %all-reduce.6.cloned.1.call-start = ((), (), s32[]{:S(2)}) async-start(), calls=%async_computation.4 | async-start | bytes 8388608 | tf_op jit(solution)/shard_map/psum | solution.py:39
  384.7 15.1 %copy-start.1 = (bf16[1152,576]{0,1:T(8,128)(2,1)S(1)}, bf16[1152,576]{0,1:T(8,128)(2,1)}, u32[]{:S(2)}) copy-start(bf16[1152,576]{0,1:T(8,128)(2,1)} %param.11) | copy-start | bytes 3981316
Sparse Core Ops, SparseCore 0:
  9.5 63.4 all-gather.2
  147.3 82.8 all-reduce.3
  246.3 20.3 reduce-scatter.1
  293.4 83.6 all-reduce.5
